TPU v7x, 32 devices: a whole 2x2x4 slice. The times are simulated.
32 devices in a mesh: leaf: 8 (over z, y), fsdp: 4 (over x, core).
Axes of the slice: x: 2, y: 2, z: 4, core: 2. Of those that a mesh axis runs over, the one named last changes fastest.
Arguments:
- hidden: bfloat16 [4, 2048, 768], P('fsdp', 'leaf'), may hold values from -6 to 6
- noise_mask: int32 [4, 2048], P('fsdp', 'leaf'), may hold values 0 or 1
- seg_blocks: int32 [4, 128], P('fsdp'), may hold values from 0 to 12, as said below
- parents: int32 [4, 13], P('fsdp'), may hold values from 0 to 4, as said below
- ln1_gain: bfloat16 [768], P(('leaf', 'fsdp')), may hold values from 0.099609375 to 1.8984375
- w_qkv: bfloat16 [768, 2304], P(('leaf', 'fsdp')), may hold values from -0.21875 to 0.21875
- w_out: bfloat16 [768, 768], P(('leaf', 'fsdp')), may hold values from -3.5 to 3.5
- ln2_gain: bfloat16 [768], P(('leaf', 'fsdp')), may hold values from 0.099609375 to 1.8984375
- w_up: bfloat16 [768, 3072], P(('leaf', 'fsdp')), may hold values from -0.21875 to 0.21875
- up_bias: bfloat16 [3072], P(('leaf', 'fsdp')), may hold values from -3 to 3
- w_down: bfloat16 [3072, 768], P(('leaf', 'fsdp')), may hold values from -0.109375 to 0.109375
- down_bias: bfloat16 [768], P(('leaf', 'fsdp')), may hold values from -2 to 2
- mask_embed: bfloat16 [768], P(('leaf', 'fsdp')), may hold values from -5 to 5
- cotangent: bfloat16 [4, 2, 2048, 768], P('fsdp', None, 'leaf'), may hold values from -6 to 6
Outputs:
- output: bfloat16 [4, 2, 2048, 768], P('fsdp', None, 'leaf')
- grad_hidden: bfloat16 [4, 2048, 768], P('fsdp', 'leaf')
- grad_ln1_gain: float32 [768], P(('leaf', 'fsdp'))
- grad_w_qkv: float32 [768, 2304], P(('leaf', 'fsdp'))
- grad_w_out: float32 [768, 768], P(('leaf', 'fsdp'))
- grad_ln2_gain: float32 [768], P(('leaf', 'fsdp'))
- grad_w_up: float32 [768, 3072], P(('leaf', 'fsdp'))
- grad_up_bias: float32 [3072], P(('leaf', 'fsdp'))
- grad_w_down: float32 [3072, 768], P(('leaf', 'fsdp'))
- grad_down_bias: float32 [768], P(('leaf', 'fsdp'))
- grad_mask_embed: float32 [768], P(('leaf', 'fsdp'))
Inputs may be any that keep to these rules, and one draw needn't show every extreme that they name: `seg_blocks`: segment numbers never fall along a tree; segment 0 holds the first 64 blocks (rounded down); every other segment has one block or more; the last segment ends the tree. `parents`: segment 0 is the trunk with parent 0; segments 1 to 4 have parent 0; each of them is the parent of exactly 2 of the segments above 4.
All inputs are finite; a program needn't handle non-finite values. No bound on the sum of `noise_mask` on one device may be relied on, other than what follows from the above.
Results may differ from a plain program's by a relative error of at most 0.015.
Values may be sent and summed in bfloat16 or wider, within the bound.
No kernel may reach another device: no remote copies, remote signals or barrier semaphores. Data moves between devices by JAX's collectives and lax.ppermute only.
A program may use at most 256 MiB of HBM per device.

v0:
```python
import math
import jax
import jax.numpy as jnp
from jax import lax
from jax.sharding import PartitionSpec as P

HEAD_DIM = 64
BLOCK = 16
NEG_FILL = -1000000000.0
EPSILON = 1e-05


def look_up(table, indices):
    slots = jnp.arange(table.shape[0], dtype=jnp.int32)
    hits = indices[..., None] == slots
    return jnp.sum(jnp.where(hits, table, 0), axis=-1)


def tree_layout(seg_row, parent_row):
    slots = jnp.arange(parent_row.shape[0], dtype=jnp.int32)
    seg_lengths = jnp.sum((seg_row[:, None] == slots).astype(jnp.int32), axis=0)
    seg_starts = jnp.cumsum(seg_lengths) - seg_lengths
    grand_parent = look_up(parent_row, parent_row)
    offsets = jnp.where(slots > 0, look_up(seg_lengths, parent_row), 0) + jnp.where(
        parent_row > 0, look_up(seg_lengths, grand_parent), 0
    )
    block_ids = jnp.arange(seg_row.shape[0], dtype=jnp.int32)
    path_block = look_up(offsets, seg_row) + block_ids - look_up(seg_starts, seg_row)
    return (path_block, look_up(parent_row, seg_row), look_up(grand_parent, seg_row))


def layer_norm(values, gain):
    centred = values - jnp.mean(values, axis=-1, keepdims=True)
    spread = jnp.mean(centred * centred, axis=-1, keepdims=True)
    return centred * lax.rsqrt(spread + EPSILON) * gain


def gelu_tanh(values):
    return jax.nn.gelu(values, approximate=True)


def rotate(values, cosine, sine):
    half = values.shape[-1] // 2
    first = values[..., :half]
    second = values[..., half:]
    return jnp.concatenate(
        [first * cosine - second * sine, second * cosine + first * sine], axis=-1
    )


def to_heads(values, heads):
    return values.reshape(values.shape[0], heads, HEAD_DIM).transpose(1, 0, 2)


def from_heads(values):
    return values.transpose(1, 0, 2).reshape(values.shape[1], values.shape[0] * values.shape[2])


def shards(
    hidden,
    noise_mask,
    seg_blocks,
    parents,
    ln1_gain,
    w_qkv,
    w_out,
    ln2_gain,
    w_up,
    up_bias,
    w_down,
    down_bias,
    mask_embed,
    cotangent,
):
    gathered = (
        lax.all_gather(ln1_gain, ("leaf", "fsdp"), axis=0, tiled=True),
        lax.all_gather(w_qkv, ("leaf", "fsdp"), axis=0, tiled=True),
        lax.all_gather(w_out, ("leaf", "fsdp"), axis=0, tiled=True),
        lax.all_gather(ln2_gain, ("leaf", "fsdp"), axis=0, tiled=True),
        lax.all_gather(w_up, ("leaf", "fsdp"), axis=0, tiled=True),
        lax.all_gather(up_bias, ("leaf", "fsdp"), axis=0, tiled=True),
        lax.all_gather(w_down, ("leaf", "fsdp"), axis=0, tiled=True),
        lax.all_gather(down_bias, ("leaf", "fsdp"), axis=0, tiled=True),
        lax.all_gather(mask_embed, ("leaf", "fsdp"), axis=0, tiled=True),
    )
    gain_one, qkv_w, out_w, gain_two, up_w, up_b, down_w, down_b, embed = gathered
    rows_dev = hidden.shape[1]
    width = hidden.shape[2]
    heads = width // HEAD_DIM
    blocks_dev = rows_dev // BLOCK
    leaf_rank = lax.axis_index("leaf")
    seg_row = seg_blocks[0]
    path_block, first_up, second_up = tree_layout(seg_row, parents[0])
    first_block = leaf_rank * blocks_dev
    own_seg = lax.dynamic_slice_in_dim(seg_row, first_block, blocks_dev)
    own_path = lax.dynamic_slice_in_dim(path_block, first_block, blocks_dev)
    own_first = lax.dynamic_slice_in_dim(first_up, first_block, blocks_dev)
    own_second = lax.dynamic_slice_in_dim(second_up, first_block, blocks_dev)
    related = (
        (seg_row[None, :] == own_seg[:, None])
        | (seg_row[None, :] == own_first[:, None])
        | (seg_row[None, :] == own_second[:, None])
    )
    clean_ok = related & (path_block[None, :] <= own_path[:, None])
    noisy_ok = related & (path_block[None, :] < own_path[:, None])
    clean_tok = jnp.repeat(jnp.repeat(clean_ok, BLOCK, axis=0), BLOCK, axis=1)
    noisy_tok = jnp.repeat(jnp.repeat(noisy_ok, BLOCK, axis=0), BLOCK, axis=1)
    row_block = jnp.arange(rows_dev, dtype=jnp.int32) // BLOCK
    same_block = row_block[:, None] == row_block[None, :]
    mask_all = jnp.concatenate(
        [
            jnp.concatenate([clean_tok, jnp.zeros_like(same_block)], axis=1),
            jnp.concatenate([noisy_tok, same_block], axis=1),
        ],
        axis=0,
    )
    offsets_in = jnp.arange(BLOCK, dtype=jnp.int32)
    positions = (own_path[:, None] * BLOCK + offsets_in).reshape(rows_dev).astype(jnp.float32)
    positions = jnp.concatenate([positions, positions])
    freqs = jnp.exp(
        jnp.arange(HEAD_DIM // 2, dtype=jnp.float32) * (-math.log(10000.0) / (HEAD_DIM // 2))
    )
    angles = positions[:, None, None] * freqs
    cosine = jnp.cos(angles)
    sine = jnp.sin(angles)
    clean = hidden[0].astype(jnp.float32)
    masked = (noise_mask[0] == 1)[:, None]
    noisy = jnp.where(masked, embed.astype(jnp.float32)[None, :], clean)
    stream = jnp.concatenate([clean, noisy], axis=0)
    gain_one_f = gain_one.astype(jnp.float32)
    gain_two_f = gain_two.astype(jnp.float32)
    normed_one = layer_norm(stream, gain_one_f).astype(jnp.bfloat16)
    projected = jnp.dot(normed_one, qkv_w, preferred_element_type=jnp.float32)
    query = rotate(
        projected[:, :width].reshape(2 * rows_dev, heads, HEAD_DIM), cosine, sine
    ).reshape(2 * rows_dev, width)
    keyed = rotate(
        projected[:, width : 2 * width].reshape(2 * rows_dev, heads, HEAD_DIM), cosine, sine
    ).reshape(2 * rows_dev, width)
    query_low = query.astype(jnp.bfloat16)
    key_low = keyed.astype(jnp.bfloat16)
    value_low = projected[:, 2 * width :].astype(jnp.bfloat16)
    tree_keys, tree_values = (
        lax.all_gather(key_low[:rows_dev], "leaf", axis=0, tiled=True),
        lax.all_gather(value_low[:rows_dev], "leaf", axis=0, tiled=True),
    )
    tree_tok = tree_keys.shape[0]
    keys_all = jnp.concatenate([tree_keys, key_low[rows_dev:]], axis=0)
    values_all = jnp.concatenate([tree_values, value_low[rows_dev:]], axis=0)
    q_heads = to_heads(query_low, heads)

    def head_forward(operands):
        q_head, k_head, v_head = operands
        raw = jnp.einsum("qd,kd->qk", q_head, k_head, preferred_element_type=jnp.float32) * 0.125
        scores = jnp.where(mask_all, raw, NEG_FILL)
        top_score = jnp.max(scores, axis=-1, keepdims=True)
        expd = jnp.exp(scores - top_score)
        total = jnp.sum(expd, axis=-1, keepdims=True)
        probs = (expd / total).astype(jnp.bfloat16)
        return (
            jnp.dot(probs, v_head, preferred_element_type=jnp.float32),
            top_score + jnp.log(total),
        )

    attended, log_norm = lax.map(
        head_forward, (q_heads, to_heads(keys_all, heads), to_heads(values_all, heads))
    )
    mixed_low = from_heads(attended).astype(jnp.bfloat16)
    after = stream + jnp.dot(mixed_low, out_w, preferred_element_type=jnp.float32)
    normed_two = layer_norm(after, gain_two_f).astype(jnp.bfloat16)
    pre_act = jnp.dot(normed_two, up_w, preferred_element_type=jnp.float32) + up_b.astype(
        jnp.float32
    )
    activated = gelu_tanh(pre_act).astype(jnp.bfloat16)
    result = (
        after
        + jnp.dot(activated, down_w, preferred_element_type=jnp.float32)
        + down_b.astype(jnp.float32)
    )
    output = result.astype(jnp.bfloat16).reshape(1, 2, rows_dev, width)
    regathered = (
        lax.all_gather(ln1_gain, ("leaf", "fsdp"), axis=0, tiled=True),
        lax.all_gather(w_qkv, ("leaf", "fsdp"), axis=0, tiled=True),
        lax.all_gather(w_out, ("leaf", "fsdp"), axis=0, tiled=True),
        lax.all_gather(ln2_gain, ("leaf", "fsdp"), axis=0, tiled=True),
        lax.all_gather(w_up, ("leaf", "fsdp"), axis=0, tiled=True),
        lax.all_gather(up_bias, ("leaf", "fsdp"), axis=0, tiled=True),
        lax.all_gather(w_down, ("leaf", "fsdp"), axis=0, tiled=True),
        lax.all_gather(down_bias, ("leaf", "fsdp"), axis=0, tiled=True),
        lax.all_gather(mask_embed, ("leaf", "fsdp"), axis=0, tiled=True),
    )
    qkv_back, out_back, up_back, down_back = (
        regathered[1],
        regathered[2],
        regathered[4],
        regathered[6],
    )
    grad_out = cotangent[0].astype(jnp.float32).reshape(2 * rows_dev, width)
    grad_two = grad_out.astype(jnp.bfloat16)
    grad_down_b = jnp.sum(grad_two.astype(jnp.float32), axis=0)
    grad_down_w = jnp.einsum("rf,rd->fd", activated, grad_two, preferred_element_type=jnp.float32)
    grad_act = jnp.einsum("rd,fd->rf", grad_two, down_back, preferred_element_type=jnp.float32)
    gelu_out, gelu_back = jax.vjp(gelu_tanh, pre_act)
    grad_pre = gelu_back(grad_act)[0].astype(jnp.bfloat16)
    grad_up_b = jnp.sum(grad_pre.astype(jnp.float32), axis=0)
    grad_up_w = jnp.einsum("rd,rf->df", normed_two, grad_pre, preferred_element_type=jnp.float32)
    grad_normed_two = jnp.einsum("rf,df->rd", grad_pre, up_back, preferred_element_type=jnp.float32)
    norm_out, norm_back = jax.vjp(layer_norm, after, gain_two_f)
    grad_after_ln, grad_gain_two = norm_back(grad_normed_two)
    grad_after = grad_out + grad_after_ln
    grad_one = grad_after.astype(jnp.bfloat16)
    grad_out_w = jnp.einsum("rd,re->de", mixed_low, grad_one, preferred_element_type=jnp.float32)
    grad_mixed = jnp.einsum(
        "re,de->rd", grad_one, out_back, preferred_element_type=jnp.float32
    ).astype(jnp.bfloat16)
    back_keys, back_values = (
        lax.all_gather(key_low[:rows_dev], "leaf", axis=0, tiled=True),
        lax.all_gather(value_low[:rows_dev], "leaf", axis=0, tiled=True),
    )
    keys_back = jnp.concatenate([back_keys, key_low[rows_dev:]], axis=0)
    values_back = jnp.concatenate([back_values, value_low[rows_dev:]], axis=0)

    def head_backward(operands):
        q_head, k_head, v_head, g_head, norm_head = operands
        raw = jnp.einsum("qd,kd->qk", q_head, k_head, preferred_element_type=jnp.float32) * 0.125
        scores = jnp.where(mask_all, raw, NEG_FILL)
        probs = jnp.exp(scores - norm_head)
        grad_v = jnp.einsum(
            "qk,qd->kd", probs.astype(jnp.bfloat16), g_head, preferred_element_type=jnp.float32
        )
        grad_p = jnp.einsum("qd,kd->qk", g_head, v_head, preferred_element_type=jnp.float32)
        inner = jnp.sum(probs * grad_p, axis=-1, keepdims=True)
        grad_s = (probs * (grad_p - inner)).astype(jnp.bfloat16)
        grad_q = jnp.einsum("qk,kd->qd", grad_s, k_head, preferred_element_type=jnp.float32) * 0.125
        grad_k = jnp.einsum("qk,qd->kd", grad_s, q_head, preferred_element_type=jnp.float32) * 0.125
        return (grad_q, grad_k, grad_v)

    grad_q_heads, grad_k_heads, grad_v_heads = lax.map(
        head_backward,
        (
            q_heads,
            to_heads(keys_back, heads),
            to_heads(values_back, heads),
            to_heads(grad_mixed, heads),
            log_norm,
        ),
    )
    grad_query = from_heads(grad_q_heads)
    grad_keys_all = from_heads(grad_k_heads)
    grad_values_all = from_heads(grad_v_heads)
    own_key_grad, own_value_grad = (
        lax.psum_scatter(
            grad_keys_all[:tree_tok].astype(jnp.bfloat16), "leaf", scatter_dimension=0, tiled=True
        ).astype(jnp.float32),
        lax.psum_scatter(
            grad_values_all[:tree_tok].astype(jnp.bfloat16), "leaf", scatter_dimension=0, tiled=True
        ).astype(jnp.float32),
    )
    grad_key = jnp.concatenate([own_key_grad, grad_keys_all[tree_tok:]], axis=0)
    grad_value = jnp.concatenate([own_value_grad, grad_values_all[tree_tok:]], axis=0)
    grad_query = rotate(grad_query.reshape(2 * rows_dev, heads, HEAD_DIM), cosine, -sine).reshape(
        2 * rows_dev, width
    )
    grad_key = rotate(grad_key.reshape(2 * rows_dev, heads, HEAD_DIM), cosine, -sine).reshape(
        2 * rows_dev, width
    )
    grad_proj = jnp.concatenate([grad_query, grad_key, grad_value], axis=1).astype(jnp.bfloat16)
    grad_qkv_w = jnp.einsum("rd,re->de", normed_one, grad_proj, preferred_element_type=jnp.float32)
    grad_normed_one = jnp.einsum(
        "re,de->rd", grad_proj, qkv_back, preferred_element_type=jnp.float32
    )
    first_out, first_back = jax.vjp(layer_norm, stream, gain_one_f)
    grad_stream_ln, grad_gain_one = first_back(grad_normed_one)
    grad_stream = grad_after + grad_stream_ln
    grad_clean = grad_stream[:rows_dev] + jnp.where(masked, 0.0, grad_stream[rows_dev:])
    grad_embed = jnp.sum(jnp.where(masked, grad_stream[rows_dev:], 0.0), axis=0)
    summed = (
        lax.psum_scatter(grad_gain_one, ("leaf", "fsdp"), scatter_dimension=0, tiled=True),
        lax.psum_scatter(grad_qkv_w, ("leaf", "fsdp"), scatter_dimension=0, tiled=True),
        lax.psum_scatter(grad_out_w, ("leaf", "fsdp"), scatter_dimension=0, tiled=True),
        lax.psum_scatter(grad_gain_two, ("leaf", "fsdp"), scatter_dimension=0, tiled=True),
        lax.psum_scatter(grad_up_w, ("leaf", "fsdp"), scatter_dimension=0, tiled=True),
        lax.psum_scatter(grad_up_b, ("leaf", "fsdp"), scatter_dimension=0, tiled=True),
        lax.psum_scatter(grad_down_w, ("leaf", "fsdp"), scatter_dimension=0, tiled=True),
        lax.psum_scatter(grad_down_b, ("leaf", "fsdp"), scatter_dimension=0, tiled=True),
        lax.psum_scatter(grad_embed, ("leaf", "fsdp"), scatter_dimension=0, tiled=True),
    )
    return (
        output,
        grad_clean.astype(jnp.bfloat16)[None],
        summed[0],
        summed[1],
        summed[2],
        summed[3],
        summed[4],
        summed[5],
        summed[6],
        summed[7],
        summed[8],
    )


def solution(mesh):
    in_specs = (
        P("fsdp", "leaf", None),
        P("fsdp", "leaf"),
        P("fsdp", None),
        P("fsdp", None),
        P(("leaf", "fsdp")),
        P(("leaf", "fsdp"), None),
        P(("leaf", "fsdp"), None),
        P(("leaf", "fsdp")),
        P(("leaf", "fsdp"), None),
        P(("leaf", "fsdp")),
        P(("leaf", "fsdp"), None),
        P(("leaf", "fsdp")),
        P(("leaf", "fsdp")),
        P("fsdp", None, "leaf", None),
    )
    out_specs = (
        P("fsdp", None, "leaf", None),
        P("fsdp", "leaf", None),
        P(("leaf", "fsdp")),
        P(("leaf", "fsdp"), None),
        P(("leaf", "fsdp"), None),
        P(("leaf", "fsdp")),
        P(("leaf", "fsdp"), None),
        P(("leaf", "fsdp")),
        P(("leaf", "fsdp"), None),
        P(("leaf", "fsdp")),
        P(("leaf", "fsdp")),
    )
    return jax.shard_map(shards, mesh=mesh, in_specs=in_specs, out_specs=out_specs, check_vma=False)
```

profile of v0, /device:TPU:0, one launch (start us, length us, event | category | flops | bytes accessed | tf_op | source)
XLA Modules:
  0.0 1240.7 jit_solution(11994550310879820292)
XLA Ops:
  12.2 42.3 %all-reduce.12 = (bf16[768]{0:T(1024)(128)(2,1)S(1)}, bf16[768]{0:T(1024)(128)(2,1)S(1)}, bf16[768]{0:T(1024)(128)(2,1)}, bf16[768]{0:T(1024)(128)(2,1)S(1)}, bf16[3072]{0:T(1024)(128)(2,1)S(1)}) all-reduce(bf16[768]{0:T(1024)(128)(2,1)S(1)} %dynamic-update-slice.1, ...), channel_id=1, replica_groups=mesh['leaf'=8,'fsdp'=4] {'leaf','fsdp'}, use_global_device_ids=true, to_apply=%add.2 | all-reduce | flops 6144 | bytes 24576
  58.5 15.2 %all-gather.7.cloned.1.call-done = bf16[768,2304]{1,0:T(8,128)(2,1)} async-done(((bf16[24,2304]{1,0:T(8,128)(2,1)}), bf16[768,2304]{1,0:T(8,128)(2,1)}) %all-gather.7.cloned.1.call-update) | async-done | bytes 3538960 | tf_op jit(solution)/shard_map/all_gather | solution.py:77
  73.8 6.2 fusion.73
  83.0 3.9 fusion.71
  88.9 3.0 copy.76
  91.9 2.7 subtract_convert_fusion.2
  105.6 34.7 %all-gather.11.cloned.1.call-done = bf16[2048,768]{1,0:T(8,128)(2,1)} async-done(((bf16[256,768]{1,0:T(8,128)(2,1)}), bf16[2048,768]{1,0:T(8,128)(2,1)}) %all-gather.11.cloned.1.call-update) | async-done | bytes 3145744 | tf_op jit(solution)/shard_map/all_gather | solution.py:145
  140.3 4.0 pad_maximum_fusion.1
  144.3 5.9 copy.80
  150.2 53.8 %all-gather.9.cloned.1.call-done = bf16[2048,768]{0,1:T(8,128)(2,1)} async-done(((bf16[256,768]{0,1:T(8,128)(2,1)}), bf16[2048,768]{0,1:T(8,128)(2,1)}) %all-gather.9.cloned.1.call-update) | async-done | bytes 3145744 | tf_op jit(solution)/shard_map/all_gather | solution.py:144
  204.1 4.0 pad_maximum_fusion
  208.1 7.9 copy.82
  216.0 8.0 copy.84
  224.0 69.5 %while.28 = (s32[]{:T(128)}, bf16[12,512,64]{1,2,0:T(8,128)(2,1)S(1)}, f32[12,512,1]{1,2,0:T(1,128)}, bf16[12,512,64]{2,1,0:T(8,128)(2,1)}, bf16[12,2304,64]{2,1...) while((s32[]{:T(128)}, ...), condition=%wide.region_14.15_spmd.clone, body=%wide.region_11.14_spmd.sunk.clone | while | flops 311426560 | bytes 16799832 | solution.py:165
  293.5 2.5 fusion.74
  297.5 27.0 %all-gather.15.cloned.1.call-done = bf16[768,3072]{1,0:T(8,128)(2,1)} async-done(((bf16[24,3072]{1,0:T(8,128)(2,1)}), bf16[768,3072]{1,0:T(8,128)(2,1)}) %all-gather.15.cloned.1.call-update) | async-done | bytes 4718608 | tf_op jit(solution)/shard_map/all_gather | solution.py:80
  324.5 8.2 fusion.64
  332.7 57.0 %all-gather.17.cloned.1.call-done = bf16[3072,768]{1,0:T(8,128)(2,1)} async-done(((bf16[96,768]{1,0:T(8,128)(2,1)}), bf16[3072,768]{1,0:T(8,128)(2,1)}) %all-gather.17.cloned.1.call-update) | async-done | bytes 4718608 | tf_op jit(solution)/shard_map/all_gather | solution.py:82
  389.7 9.9 convert_reduce_fusion
  399.6 3.4 multiply_reduce_fusion.1
  410.1 154.7 %while.29 = (s32[]{:T(128)}, f32[12,512,64]{1,2,0:T(8,128)}, f32[12,2304,64]{1,2,0:T(8,128)}, bf16[12,2304,64]{1,2,0:T(8,128)(2,1)}, bf16[12,512,64]{2,1,0:T(8,1...) while((s32[]{:T(128)}, f32[12,512,64]{1,2,0:T(8,128)}, ...), condition=%wide.region_21.22_spmd.clone, body=%wide.region_19.21_spmd.sunk.clone | while | flops 765771264 | bytes 40057968 | solution.py:238
  412.7 2.8 multiply_reduce_fusion.9
  418.1 2.5 fusion.139
  425.5 2.8 multiply_reduce_fusion.9
  430.9 2.5 fusion.139
  438.4 2.8 multiply_reduce_fusion.9
  443.8 2.6 fusion.139
  451.3 2.8 multiply_reduce_fusion.9
  456.7 2.6 fusion.139
  464.2 2.8 multiply_reduce_fusion.9
  469.6 2.6 fusion.139
  477.0 2.8 multiply_reduce_fusion.9
  482.5 2.6 fusion.139
  485.0 2.3 fusion.140
  489.9 2.8 multiply_reduce_fusion.9
  495.4 2.6 fusion.139
  502.8 2.8 multiply_reduce_fusion.9
  508.2 2.6 fusion.139
  510.8 2.3 fusion.140
  515.7 2.8 multiply_reduce_fusion.9
  521.1 2.6 fusion.139
  528.6 2.8 multiply_reduce_fusion.9
  534.0 2.6 fusion.139
  541.5 2.8 multiply_reduce_fusion.9
  546.9 2.6 fusion.139
  549.5 2.4 fusion.140
  554.4 2.8 multiply_reduce_fusion.9
  559.8 2.6 fusion.139
  562.4 2.3 fusion.140
  564.7 4.9 slice.169
  569.7 3.9 slice.123
  574.8 3.5 fusion.75
  578.3 10.1 fusion.66
  589.9 7.2 fusion.63
  601.2 42.4 %reduce-scatter.7.cloned.1.call-done = bf16[256,768]{0,1:T(8,128)(2,1)} async-done(((bf16[2048,768]{0,1:T(8,128)(2,1)}), bf16[256,768]{0,1:T(8,128)(2,1)}) %reduce-scatter.7.cloned.1.call-update) | async-done | bytes 393232 | tf_op jit(solution)/shard_map/reduce_scatter | solution.py:252
  648.9 72.4 %reduce-scatter.9.cloned.1.call-done = bf16[256,768]{0,1:T(8,128)(2,1)} async-done(((bf16[2048,768]{0,1:T(8,128)(2,1)}), bf16[256,768]{0,1:T(8,128)(2,1)}) %reduce-scatter.9.cloned.1.call-update) | async-done | bytes 393232 | tf_op jit(solution)/shard_map/reduce_scatter | solution.py:255
  721.3 6.7 fusion.52
  730.6 9.3 add_convert_fusion
  739.9 2.4 multiply_reduce_fusion.2
  745.6 40.2 %all-reduce.11 = (f32[768]{0:T(1024)S(1)}, f32[768]{0:T(1024)S(1)}, f32[3072]{0:T(1024)S(1)}, f32[768]{0:T(1024)S(1)}, f32[768]{0:T(1024)S(1)}) all-reduce(f32[768]{0:T(1024)S(1)} %get-tuple-element.195, f32[768]{0:T(1024)S(1)} %copy-done.34, f32[3072]{0:T(1024)S(1)} %copy-done.31, ...), channel_id=4, replica_groups=mesh['leaf'=8,'fsdp'=4] {'leaf','fsdp'}, use_global_device_ids=true, to_apply=%region_27.28.clone | all-reduce | flops 6144 | bytes 49152
  788.8 36.7 %reduce-scatter.13.cloned.1.call-done = f32[24,768]{1,0:T(8,128)} async-done(((f32[768,768]{1,0:T(8,128)}), f32[24,768]{1,0:T(8,128)}) %reduce-scatter.13.cloned.1.call-update) | async-done | bytes 73744 | tf_op jit(solution)/shard_map/reduce_scatter | solution.py:280
  825.5 141.8 %reduce-scatter.17.cloned.1.call-done = f32[96,768]{1,0:T(8,128)} async-done(((f32[3072,768]{1,0:T(8,128)}), f32[96,768]{1,0:T(8,128)}) %reduce-scatter.17.cloned.1.call-update) | async-done | bytes 294928 | tf_op jit(solution)/shard_map/reduce_scatter | solution.py:284
  967.3 141.1 %reduce-scatter.15.cloned.1.call-done = f32[24,3072]{1,0:T(8,128)} async-done(((f32[768,3072]{1,0:T(8,128)}), f32[24,3072]{1,0:T(8,128)}) %reduce-scatter.15.cloned.1.call-update) | async-done | bytes 294928 | tf_op jit(solution)/shard_map/reduce_scatter | solution.py:282
  1108.4 125.2 %reduce-scatter.11.cloned.1.call-done = f32[24,2304]{1,0:T(8,128)} async-done(((f32[768,2304]{1,0:T(8,128)}), f32[24,2304]{1,0:T(8,128)}) %reduce-scatter.11.cloned.1.call-update) | async-done | bytes 221200 | tf_op jit(solution)/shard_map/reduce_scatter | solution.py:279
  (308 shorter events, 203.7 us)
Async XLA Ops:
  7.2 66.6 %all-gather.7.cloned.1.call-start = ((), (), s32[]{:S(2)}) async-start(), calls=%async_computation.6 | async-start | bytes 3649536 | tf_op jit(solution)/shard_map/all_gather | solution.py:77
  7.9 132.4 %all-gather.11.cloned.1.call-start = ((), (), s32[]{:S(2)}) async-start(), calls=%async_computation.8 | async-start | bytes 3538944 | tf_op jit(solution)/shard_map/all_gather | solution.py:145
  54.5 19.2 %copy-start.26 = (f32[768]{0:T(1024)}, f32[768]{0:T(1024)S(1)}, u32[]{:S(2)}) copy-start(f32[768]{0:T(1024)S(1)} %convert_element_type.105) | copy-start | bytes 9220
  55.2 2.7 copy-start.35
  57.6 22.4 %copy-start.22 = (f32[512]{0:T(512)}, f32[512]{0:T(512)S(1)}, u32[]{:S(2)}) copy-start(f32[512]{0:T(512)S(1)} %broadcast_multiply_fusion.1) | copy-start | bytes 6148
  57.9 0.6 copy-start.28
  58.5 21.5 %copy-start.24 = (f32[512]{0:T(512)}, f32[512]{0:T(512)S(1)}, u32[]{:S(2)}) copy-start(f32[512]{0:T(512)S(1)} %fusion.57) | copy-start | bytes 6148
  58.5 22.5 %copy-start.37 = (s32[1,128]{1,0:T(1,128)S(1)}, s32[1,128]{1,0:T(1,128)}, u32[]{:S(2)}) copy-start(s32[1,128]{1,0:T(1,128)} %param.20) | copy-start | bytes 1540
  58.5 22.8 %copy-start.33 = (s32[1,13]{1,0:T(1,128)S(1)}, s32[1,13]{1,0:T(1,128)}, u32[]{:S(2)}) copy-start(s32[1,13]{1,0:T(1,128)} %param.21) | copy-start | bytes 160
  81.0 123.1 %all-gather.9.cloned.1.call-start = ((), (), s32[]{:S(2)}) async-start(), calls=%async_computation.7 | async-start | bytes 3538944 | tf_op jit(solution)/shard_map/all_gather | solution.py:144
  83.0 8.9 copy-start.18
  95.6 197.8 %all-gather.13.cloned.1.call-start = ((), (), s32[]{:S(2)}) async-start(), calls=%async_computation.9 | async-start | bytes 1216512 | tf_op jit(solution)/shard_map/all_gather | solution.py:78
  96.2 228.2 %all-gather.15.cloned.1.call-start = ((), (), s32[]{:S(2)}) async-start(), calls=%async_computation.10 | async-start | bytes 4866048 | tf_op jit(solution)/shard_map/all_gather | solution.py:80
  96.8 292.9 %all-gather.17.cloned.1.call-start = ((), (), s32[]{:S(2)}) async-start(), calls=%async_computation.11 | async-start | bytes 4866048 | tf_op jit(solution)/shard_map/all_gather | solution.py:82
  97.4 546.2 %reduce-scatter.7.cloned.1.call-start = ((), (), s32[]{:S(2)}) async-start(), calls=%async_computation.12 | async-start | bytes 3538944 | tf_op jit(solution)/shard_map/reduce_scatter | solution.py:252
  100.4 3.5 copy-start.14
  100.5 3.5 copy-start.15
  144.3 59.8 %copy-start.13 = (bf16[256,12,64]{0,2,1:T(8,128)(2,1)S(1)}, bf16[256,12,64]{0,2,1:T(8,128)(2,1)}, u32[]{:S(2)}) copy-start(bf16[256,12,64]{0,2,1:T(8,128)(2,1)} %get-tuple-element.274) | copy-start | bytes 1179652
  216.0 8.0 copy-start.8
  293.4 2.5 copy-start.9
  295.9 1.2 copy-start.2
  297.4 92.3 %copy-start.5 = (bf16[1,2,256,768]{3,2,1,0:T(8,128)(2,1)S(1)}, bf16[1,2,256,768]{3,2,1,0:T(8,128)(2,1)}, u32[]{:S(2)}) copy-start(bf16[1,2,256,768]{3,2,1,0:T(8,128)(2,1)} %param.31) | copy-start | bytes 2359300
  389.7 9.9 copy-start.3
  389.7 9.9 copy-start.38
  399.6 3.4 copy-start.12
  403.7 1.2 copy-start
  403.7 2.3 copy-start.39
  405.2 0.9 copy-start.11
  569.7 151.7 %reduce-scatter.9.cloned.1.call-start = ((), (), s32[]{:S(2)}) async-start(), calls=%async_computation.13 | async-start | bytes 3538944 | tf_op jit(solution)/shard_map/reduce_scatter | solution.py:255
  573.6 1.1 copy-start.10
  573.7 4.6 copy-start.32
  573.7 251.8 %reduce-scatter.13.cloned.1.call-start = ((), (), s32[]{:S(2)}) async-start(), calls=%async_computation.15 | async-start | bytes 2433024 | tf_op jit(solution)/shard_map/reduce_scatter | solution.py:280
  578.3 389.1 %reduce-scatter.17.cloned.1.call-start = ((), (), s32[]{:S(2)}) async-start(), calls=%async_computation.17 | async-start | bytes 9732096 | tf_op jit(solution)/shard_map/reduce_scatter | solution.py:284
  588.4 1.4 copy-start.4
  588.5 520.0 %reduce-scatter.15.cloned.1.call-start = ((), (), s32[]{:S(2)}) async-start(), calls=%async_computation.16 | async-start | bytes 9732096 | tf_op jit(solution)/shard_map/reduce_scatter | solution.py:282
  597.0 47.6 %copy-start.19 = (f32[512,32]{0,1:T(8,128)S(1)}, f32[512,32]{0,1:T(8,128)}, u32[]{:S(2)}) copy-start(f32[512,32]{0,1:T(8,128)} %copy-done.18) | copy-start | bytes 196612
  597.1 47.6 %copy-start.21 = (f32[512,32]{0,1:T(8,128)S(1)}, f32[512,32]{0,1:T(8,128)}, u32[]{:S(2)}) copy-start(f32[512,32]{0,1:T(8,128)} %get-tuple-element.281) | copy-start | bytes 196612
  597.1 636.5 %reduce-scatter.11.cloned.1.call-start = ((), (), s32[]{:S(2)}) async-start(), calls=%async_computation.14 | async-start | bytes 7299072 | tf_op jit(solution)/shard_map/reduce_scatter | solution.py:279
  646.9 74.4 %copy-start.20 = (bf16[256,12,64]{0,2,1:T(8,128)(2,1)S(1)}, bf16[256,12,64]{0,2,1:T(8,128)(2,1)}, u32[]{:S(2)}) copy-start(bf16[256,12,64]{0,2,1:T(8,128)(2,1)} %slice.124) | copy-start | bytes 1179652
  646.9 74.4 %copy-start.23 = (f32[512]{0:T(512)S(1)}, f32[512]{0:T(512)}, u32[]{:S(2)}) copy-start(f32[512]{0:T(512)} %copy-done.22) | copy-start | bytes 6148
  647.0 74.4 %copy-start.25 = (f32[512]{0:T(512)S(1)}, f32[512]{0:T(512)}, u32[]{:S(2)}) copy-start(f32[512]{0:T(512)} %copy-done.24) | copy-start | bytes 6148
  647.0 74.4 %copy-start.27 = (f32[768]{0:T(1024)S(1)}, f32[768]{0:T(1024)}, u32[]{:S(2)}) copy-start(f32[768]{0:T(1024)} %copy-done.26) | copy-start | bytes 9220
  730.6 9.3 copy-start.7
  730.6 9.3 copy-start.16
  730.6 9.3 copy-start.17
  730.6 9.3 copy-start.40
  739.9 2.5 copy-start.29
  742.4 1.4 copy-start.1
  742.4 1.6 copy-start.6
  744.0 0.7 copy-start.36
  744.0 1.6 copy-start.30
  744.0 1.6 copy-start.31
  744.0 1.6 copy-start.34
Sparse Core Ops, SparseCore 0:
  10.9 62.7 all-gather.6
  81.1 59.1 all-gather.10
  142.3 61.6 all-gather.8
  206.8 52.2 all-gather.12
  261.9 62.5 all-gather.14
  327.2 62.4 all-gather.16
  569.8 73.7 reduce-scatter.6
  647.2 74.0 reduce-scatter.8
  727.2 98.2 reduce-scatter.12
  832.8 134.4 reduce-scatter.16
  973.8 134.5 reduce-scatter.14
  1115.5 118.0 reduce-scatter.10
where the time goes:
time: 1250 us; the launch traced here: 1240 us
  waiting for transfers between devices  750 us (60%)
  matrix products  264 us (21%)
  blocking collectives  82.6 us (7%)
  local copies, waits for them, and re-layouts  80.2 us (6%)
  other arithmetic  47 us (4%)
  between operations  15 us (1%)
    reduce_scatter x1, waiting for transfers between devices, shards(): lax.psum_scatter(grad_down_w, ('leaf', 'fsdp'), scatter_dimension=0, tile...  142 us
    reduce_scatter x1, waiting for transfers between devices, shards(): lax.psum_scatter(grad_up_w, ('leaf', 'fsdp'), scatter_dimension=0, tiled=...  141 us
    reduce_scatter x1, waiting for transfers between devices, shards(): lax.psum_scatter(grad_qkv_w, ('leaf', 'fsdp'), scatter_dimension=0, tiled...  125 us
    unnamed x2, blocking collectives  82.6 us
    reduce_scatter x1, waiting for transfers between devices, shards(): lax.psum_scatter(grad_values_all[:tree_tok].astype(jnp.bfloat16), 'leaf',...  72.4 us
    all_gather x1, waiting for transfers between devices, shards(): lax.all_gather(w_down, ('leaf', 'fsdp'), axis=0, tiled=True)  57 us
    all_gather x1, waiting for transfers between devices, shards(): lax.all_gather(key_low[:rows_dev], 'leaf', axis=0, tiled=True)  53.8 us
    reduce_scatter x1, waiting for transfers between devices, shards(): lax.psum_scatter(grad_keys_all[:tree_tok].astype(jnp.bfloat16), 'leaf', s...  42.4 us
  transfers between devices with their start and end apart: 12, of which 11 were waited for; matrix products, arithmetic and copies ran while one was open for 16% of the time, Pallas kernels for 0%

commit v1 on v0

--- a/solution.py
+++ b/solution.py
@@ -8,6 +8,24 @@
 BLOCK = 16
 NEG_FILL = -1000000000.0
 EPSILON = 1e-05
+
+
+def gather_around(shard, axis, dim):
+    ways, here, step = (lax.axis_size(axis), lax.axis_index(axis), shard.shape[dim])
+    shape = [n * ways if d == dim else n for d, n in enumerate(shard.shape)]
+    full = lax.dynamic_update_slice_in_dim(
+        jnp.zeros(shape, shard.dtype), shard, here * step, axis=dim
+    )
+    going_up = going_down = shard
+    for far in range(1, ways // 2 + 1):
+        going_up = lax.ppermute(going_up, axis, [(d, (d + 1) % ways) for d in range(ways)])
+        full = lax.dynamic_update_slice_in_dim(full, going_up, (here - far) % ways * step, axis=dim)
+        if 2 * far < ways:
+            going_down = lax.ppermute(going_down, axis, [(d, (d - 1) % ways) for d in range(ways)])
+            full = lax.dynamic_update_slice_in_dim(
+                full, going_down, (here + far) % ways * step, axis=dim
+            )
+    return full
 
 
 def look_up(table, indices):
@@ -142,7 +160,7 @@
     value_low = projected[:, 2 * width :].astype(jnp.bfloat16)
     tree_keys, tree_values = (
         lax.all_gather(key_low[:rows_dev], "leaf", axis=0, tiled=True),
-        lax.all_gather(value_low[:rows_dev], "leaf", axis=0, tiled=True),
+        gather_around(value_low[:rows_dev], "leaf", 0),
     )
     tree_tok = tree_keys.shape[0]
     keys_all = jnp.concatenate([tree_keys, key_low[rows_dev:]], axis=0)

time: 1250 us -> 1310 us (1.048)
  matrix products: 264 us -> 278 us
  starting transfers between devices: 1.16 us -> 15 us
  local copies, waits for them, and re-layouts: 80.2 us -> 93.4 us
    all_gather x1, waiting for transfers between devices: 53.8 us -> 1.52 us  [shards(): lax.all_gather(key_low[:rows_dev], 'leaf', axis=0, tiled=True)]
    ppermute x0 -> x7, waiting for transfers between devices: none -> 47.1 us  [the longest x3 34.2 us: gather_around(): lax.ppermute(going_down, axis, [(d, (d - 1) % ways) for d in range(ways)])]
    all_gather x1, waiting for transfers between devices: 34.7 us -> 0.01 us  [shards(): lax.all_gather(value_low[:rows_dev], 'leaf', axis=0, tiled=True)]
    all_gather x1, waiting for transfers between devices: 27 us -> 61.7 us  [shards(): lax.all_gather(w_up, ('leaf', 'fsdp'), axis=0, tiled=True)]
    all_gather x1, waiting for transfers between devices: 0.01 us -> 19.3 us  [shards(): lax.all_gather(w_out, ('leaf', 'fsdp'), axis=0, tiled=True)]
    ppermute x0 -> x7, starting transfers between devices: none -> 14.3 us  [the longest x3 7.77 us: gather_around(): lax.ppermute(going_down, axis, [(d, (d - 1) % ways) for d in range(ways)])]
  transfers between devices with their start and end apart: 12 -> 19, of which waited for: 11 -> 15; matrix products, arithmetic and copies ran while one was open for 16% -> 17% of each run, Pallas kernels for 0% -> 0%
where the time goes in v1:
time: 1310 us; the launch traced here: 1300 us
  waiting for transfers between devices  759 us (58%)
  matrix products  278 us (21%)
  local copies, waits for them, and re-layouts  93.4 us (7%)
  blocking collectives  82.6 us (6%)
  other arithmetic  57.3 us (4%)
  between operations  15.2 us (1%)
  starting transfers between devices  15 us (1%)
    reduce_scatter x1, waiting for transfers between devices, shards(): lax.psum_scatter(grad_down_w, ('leaf', 'fsdp'), scatter_dimension=0, tile...  142 us
    reduce_scatter x1, waiting for transfers between devices, shards(): lax.psum_scatter(grad_up_w, ('leaf', 'fsdp'), scatter_dimension=0, tiled=...  141 us
    reduce_scatter x1, waiting for transfers between devices, shards(): lax.psum_scatter(grad_qkv_w, ('leaf', 'fsdp'), scatter_dimension=0, tiled...  126 us
    unnamed x2, blocking collectives  82.6 us
    reduce_scatter x1, waiting for transfers between devices, shards(): lax.psum_scatter(grad_values_all[:tree_tok].astype(jnp.bfloat16), 'leaf',...  72.3 us
    all_gather x1, waiting for transfers between devices, shards(): lax.all_gather(w_up, ('leaf', 'fsdp'), axis=0, tiled=True)  61.7 us
    all_gather x1, waiting for transfers between devices, shards(): lax.all_gather(w_down, ('leaf', 'fsdp'), axis=0, tiled=True)  57 us
    reduce_scatter x1, waiting for transfers between devices, shards(): lax.psum_scatter(grad_keys_all[:tree_tok].astype(jnp.bfloat16), 'leaf', s...  42.5 us
  transfers between devices with their start and end apart: 19, of which 15 were waited for; matrix products, arithmetic and copies ran while one was open for 17% of the time, Pallas kernels for 0%

profile of v1, /device:TPU:0, one launch (start us, length us, event | category | flops | bytes accessed | tf_op | source)
XLA Modules:
  0.0 1300.5 jit_solution(17583258657728697384)
XLA Ops:
  13.1 42.4 %all-reduce.12 = (bf16[768]{0:T(1024)(128)(2,1)S(1)}, bf16[768]{0:T(1024)(128)(2,1)S(1)}, bf16[768]{0:T(1024)(128)(2,1)}, bf16[768]{0:T(1024)(128)(2,1)S(1)}, bf16[3072]{0:T(1024)(128)(2,1)S(1)}) all-reduce(bf16[768]{0:T(1024)(128)(2,1)S(1)} %dynamic-update-slice.1, ...), channel_id=1, replica_groups=mesh['leaf'=8,'fsdp'=4] {'leaf','fsdp'}, use_global_device_ids=true, to_apply=%add.2 | all-reduce | flops 6144 | bytes 24576
  63.9 9.9 all-gather.7.cloned.1.call-done
  73.8 5.5 fusion.74
  83.0 3.0 copy.103
  86.1 2.7 subtract_convert_fusion.2
  93.9 3.0 collective-permute-start.1
  97.4 20.7 %collective-permute-done.1 = bf16[256,768]{1,0:T(8,128)(2,1)} collective-permute-done((bf16[256,768]{1,0:T(8,128)(2,1)}, bf16[256,768]{1,0:T(8,128)(2,1)}, u32[]{:S(2)}, u32[]{:S(2)}) %collective-permute-start.1) | collective-permute-done | bytes 393248 | tf_op jit(solution)/shard_map/ppermute | solution.py:24
  120.8 3.0 pad_add_fusion
  127.9 10.2 collective-permute-done.2
  150.0 3.6 collective-permute-start.5
  157.6 2.7 collective-permute-done.4
  160.3 3.9 collective-permute-start.6
  168.2 13.5 %collective-permute-done.5 = bf16[256,768]{1,0:T(8,128)(2,1)} collective-permute-done((bf16[256,768]{1,0:T(8,128)(2,1)}, bf16[256,768]{1,0:T(8,128)(2,1)}, u32[]{:S(2)}, u32[]{:S(2)}) %collective-permute-start.5) | collective-permute-done | bytes 393248 | tf_op jit(solution)/shard_map/ppermute | solution.py:24
  188.2 4.1 pad_maximum_fusion.1
  193.9 4.0 pad_maximum_fusion
  197.9 8.0 copy.117
  205.9 75.5 %while.28 = (s32[]{:T(128)}, bf16[12,512,64]{1,2,0:T(8,128)(2,1)}, f32[12,512,1]{1,2,0:T(1,128)}, bf16[12,512,64]{2,1,0:T(8,128)(2,1)}, bf16[12,2304,64]{2,1,0:T...) while((s32[]{:T(128)}, bf16[12,512,64]{1,2,0:T(8,128)(2,1)}, ...), condition=%wide.region_14.15_spmd.clone, body=%wide.region_11.14_spmd.sunk.clone | while | flops 311426560 | bytes 16504921 | solution.py:183
  208.8 2.7 fusion.130
  215.1 2.7 fusion.130
  221.4 2.7 fusion.130
  227.7 2.7 fusion.130
  234.0 2.7 fusion.130
  240.2 2.7 fusion.130
  246.6 2.7 fusion.130
  252.9 2.7 fusion.130
  259.1 2.7 fusion.130
  265.4 2.7 fusion.130
  271.7 2.7 fusion.130
  278.0 2.7 fusion.130
  281.3 3.9 pad_maximum_fusion.2
  285.2 5.9 copy.121
  291.1 19.3 %all-gather.11.cloned.1.call-done = bf16[768,768]{1,0:T(8,128)(2,1)} async-done(((bf16[24,768]{1,0:T(8,128)(2,1)}), bf16[768,768]{1,0:T(8,128)(2,1)}) %all-gather.11.cloned.1.call-update) | async-done | bytes 1179664 | tf_op jit(solution)/shard_map/all_gather | solution.py:96
  314.0 61.7 %all-gather.13.cloned.1.call-done = bf16[768,3072]{1,0:T(8,128)(2,1)} async-done(((bf16[24,3072]{1,0:T(8,128)(2,1)}), bf16[768,3072]{1,0:T(8,128)(2,1)}) %all-gather.13.cloned.1.call-update) | async-done | bytes 4718608 | tf_op jit(solution)/shard_map/all_gather | solution.py:98
  375.7 8.2 fusion.65
  384.0 57.0 %all-gather.15.cloned.1.call-done = bf16[3072,768]{1,0:T(8,128)(2,1)} async-done(((bf16[96,768]{1,0:T(8,128)(2,1)}), bf16[3072,768]{1,0:T(8,128)(2,1)}) %all-gather.15.cloned.1.call-update) | async-done | bytes 4718608 | tf_op jit(solution)/shard_map/all_gather | solution.py:100
  441.0 19.8 %convert_reduce_fusion = (f32[3072]{0:T(1024)}, bf16[512,3072]{1,0:T(8,128)(2,1)S(1)}) fusion(f32[512,3072]{1,0:T(8,128)} %fusion.65, f32[3072]{0:T(1024)} %convert_element_type.115, bf16[512,768]{1,0:T(8,128)(2,1)S(1)} %bitcast.189, bf16[3072,768]{1,0:T(8,128)(2,1)} %all-gather.15.cloned.1.call-done), kind=kOutput, calls=%fused_computation.64 | convolution fusion | flops 2452091904 | bytes 14966784 | tf_op jit(solution)/shard_map/rd,fd->rf/dot_general | solution.py:220
  460.8 3.4 multiply_reduce_fusion.1
  471.3 152.9 %while.29 = (s32[]{:T(128)}, f32[12,512,64]{1,2,0:T(8,128)}, f32[12,2304,64]{1,2,0:T(8,128)}, bf16[12,2304,64]{1,2,0:T(8,128)(2,1)}, bf16[12,512,64]{2,1,0:T(8,1...) while((s32[]{:T(128)}, f32[12,512,64]{1,2,0:T(8,128)}, ...), condition=%wide.region_21.22_spmd.clone, body=%wide.region_19.21_spmd.sunk.clone | while | flops 765771264 | bytes 39763056 | solution.py:256
  473.8 2.8 multiply_reduce_fusion.9
  486.6 2.8 multiply_reduce_fusion.9
  499.3 2.8 multiply_reduce_fusion.9
  512.0 2.8 multiply_reduce_fusion.9
  524.7 2.8 multiply_reduce_fusion.9
  537.5 2.8 multiply_reduce_fusion.9
  550.2 2.8 multiply_reduce_fusion.9
  562.9 2.8 multiply_reduce_fusion.9
  575.7 2.8 multiply_reduce_fusion.9
  588.4 2.8 multiply_reduce_fusion.9
  601.2 2.8 multiply_reduce_fusion.9
  614.0 2.8 multiply_reduce_fusion.9
  624.3 4.9 slice.169
  629.2 3.9 slice.123
  634.3 3.4 fusion.76
  637.8 10.0 fusion.67
  649.3 7.2 fusion.64
  660.6 42.5 %reduce-scatter.7.cloned.1.call-done = bf16[256,768]{0,1:T(8,128)(2,1)} async-done(((bf16[2048,768]{0,1:T(8,128)(2,1)}), bf16[256,768]{0,1:T(8,128)(2,1)}) %reduce-scatter.7.cloned.1.call-update) | async-done | bytes 393232 | tf_op jit(solution)/shard_map/reduce_scatter | solution.py:270
  708.4 72.3 %reduce-scatter.9.cloned.1.call-done = bf16[256,768]{0,1:T(8,128)(2,1)} async-done(((bf16[2048,768]{0,1:T(8,128)(2,1)}), bf16[256,768]{0,1:T(8,128)(2,1)}) %reduce-scatter.9.cloned.1.call-update) | async-done | bytes 393232 | tf_op jit(solution)/shard_map/reduce_scatter | solution.py:273
  780.8 6.7 fusion.52
  790.0 9.3 add_convert_fusion
  804.8 40.2 %all-reduce.11 = (f32[768]{0:T(1024)S(1)}, f32[768]{0:T(1024)S(1)}, f32[3072]{0:T(1024)S(1)}, f32[768]{0:T(1024)S(1)}, f32[768]{0:T(1024)S(1)}) all-reduce(f32[768]{0:T(1024)S(1)} %get-tuple-element.195, f32[768]{0:T(1024)S(1)} %copy-done.32, f32[3072]{0:T(1024)S(1)} %copy-done.30, ...), channel_id=4, replica_groups=mesh['leaf'=8,'fsdp'=4] {'leaf','fsdp'}, use_global_device_ids=true, to_apply=%region_27.28.clone | all-reduce | flops 6144 | bytes 49152
  848.0 36.9 %reduce-scatter.13.cloned.1.call-done = f32[24,768]{1,0:T(8,128)} async-done(((f32[768,768]{1,0:T(8,128)}), f32[24,768]{1,0:T(8,128)}) %reduce-scatter.13.cloned.1.call-update) | async-done | bytes 73744 | tf_op jit(solution)/shard_map/reduce_scatter | solution.py:298
  884.9 141.9 %reduce-scatter.17.cloned.1.call-done = f32[96,768]{1,0:T(8,128)} async-done(((f32[3072,768]{1,0:T(8,128)}), f32[96,768]{1,0:T(8,128)}) %reduce-scatter.17.cloned.1.call-update) | async-done | bytes 294928 | tf_op jit(solution)/shard_map/reduce_scatter | solution.py:302
  1026.7 141.0 %reduce-scatter.15.cloned.1.call-done = f32[24,3072]{1,0:T(8,128)} async-done(((f32[768,3072]{1,0:T(8,128)}), f32[24,3072]{1,0:T(8,128)}) %reduce-scatter.15.cloned.1.call-update) | async-done | bytes 294928 | tf_op jit(solution)/shard_map/reduce_scatter | solution.py:300
  1167.7 125.5 %reduce-scatter.11.cloned.1.call-done = f32[24,2304]{1,0:T(8,128)} async-done(((f32[768,2304]{1,0:T(8,128)}), f32[24,2304]{1,0:T(8,128)}) %reduce-scatter.11.cloned.1.call-update) | async-done | bytes 221200 | tf_op jit(solution)/shard_map/reduce_scatter | solution.py:297
  (336 shorter events, 253.1 us)
Async XLA Ops:
  7.2 66.6 %all-gather.7.cloned.1.call-start = ((), (), s32[]{:S(2)}) async-start(), calls=%async_computation.6 | async-start | bytes 3649536 | tf_op jit(solution)/shard_map/all_gather | solution.py:95
  7.9 186.0 %all-gather.9.cloned.1.call-start = ((), (), s32[]{:S(2)}) async-start(), calls=%async_computation.7 | async-start | bytes 3538944 | tf_op jit(solution)/shard_map/all_gather | solution.py:162
  55.5 23.8 %copy-start.25 = (f32[768]{0:T(1024)}, f32[768]{0:T(1024)S(1)}, u32[]{:S(2)}) copy-start(f32[768]{0:T(1024)S(1)} %convert_element_type.105) | copy-start | bytes 9220
  59.6 19.7 %copy-start.33 = (pred[256]{0:T(512)(128)(4,1)}, pred[256]{0:T(512)(128)(4,1)S(1)}, u32[]{:S(2)}) copy-start(pred[256]{0:T(512)(128)(4,1)S(1)} %compare_reduce_fusion) | copy-start | bytes 772
  62.0 17.3 %copy-start.21 = (f32[512]{0:T(512)}, f32[512]{0:T(512)S(1)}, u32[]{:S(2)}) copy-start(f32[512]{0:T(512)S(1)} %broadcast_multiply_fusion.1) | copy-start | bytes 6148
  62.3 0.6 copy-start.27
  62.9 16.4 %copy-start.23 = (f32[512]{0:T(512)}, f32[512]{0:T(512)S(1)}, u32[]{:S(2)}) copy-start(f32[512]{0:T(512)S(1)} %fusion.57) | copy-start | bytes 6148
  63.9 22.2 %copy-start.17 = (f32[512,32]{0,1:T(8,128)}, f32[512,32]{0,1:T(8,128)S(1)}, u32[]{:S(2)}) copy-start(f32[512,32]{0,1:T(8,128)S(1)} %get-tuple-element.283) | copy-start | bytes 196612
  88.8 4.8 copy-start.35
  89.8 191.5 %all-gather.17.cloned.1.call-start = ((), (), s32[]{:S(2)}) async-start(), calls=%async_computation.11 | async-start | bytes 3538944 | tf_op jit(solution)/shard_map/all_gather | solution.py:236
  91.8 218.6 %all-gather.11.cloned.1.call-start = ((), (), s32[]{:S(2)}) async-start(), calls=%async_computation.8 | async-start | bytes 1216512 | tf_op jit(solution)/shard_map/all_gather | solution.py:96
  92.4 283.3 %all-gather.13.cloned.1.call-start = ((), (), s32[]{:S(2)}) async-start(), calls=%async_computation.9 | async-start | bytes 4866048 | tf_op jit(solution)/shard_map/all_gather | solution.py:98
  93.0 348.0 %all-gather.15.cloned.1.call-start = ((), (), s32[]{:S(2)}) async-start(), calls=%async_computation.10 | async-start | bytes 4866048 | tf_op jit(solution)/shard_map/all_gather | solution.py:100
  93.6 609.5 %reduce-scatter.7.cloned.1.call-start = ((), (), s32[]{:S(2)}) async-start(), calls=%async_computation.12 | async-start | bytes 3538944 | tf_op jit(solution)/shard_map/reduce_scatter | solution.py:270
  93.9 24.2 %collective-permute-start.1 = (bf16[256,768]{1,0:T(8,128)(2,1)}, bf16[256,768]{1,0:T(8,128)(2,1)}, u32[]{:S(2)}, u32[]{:S(2)}) collective-permute-start(bf16[256,768]{1,0:T(8,128)(2,1)} %get-tuple-element.261), channel_id=1, source_target_pairs={{0,28},{4,0},{8,4},{12,8},{16,12},{20,16},{24,20},{28,24},{1,29},{... | collective-permute-start | bytes 1179656 | tf_op jit(solution)/shard_map/ppermute | solution.py:24
  96.9 22.3 %collective-permute-start = (bf16[256,768]{1,0:T(8,128)(2,1)}, bf16[256,768]{1,0:T(8,128)(2,1)}, u32[]{:S(2)}, u32[]{:S(2)}) collective-permute-start(bf16[256,768]{1,0:T(8,128)(2,1)} %get-tuple-element.261), channel_id=1, source_target_pairs={{0,4},{4,8},{8,12},{12,16},{16,20},{20,24},{24,28},{28,0},{1,5},{5... | collective-permute-start | bytes 1179656 | tf_op jit(solution)/shard_map/ppermute | solution.py:21
  118.1 31.9 %collective-permute-start.3 = (bf16[256,768]{1,0:T(8,128)(2,1)}, bf16[256,768]{1,0:T(8,128)(2,1)}, u32[]{:S(2)}, u32[]{:S(2)}) collective-permute-start(bf16[256,768]{1,0:T(8,128)(2,1)} %collective-permute-done.1), channel_id=1, source_target_pairs={{0,28},{4,0},{8,4},{12,8},{16,12},{20,16},{24,20},{28,24},{1,29},{... | collective-permute-start | bytes 1179656 | tf_op jit(solution)/shard_map/ppermute | solution.py:24
  119.2 18.8 %collective-permute-start.2 = (bf16[256,768]{1,0:T(8,128)(2,1)}, bf16[256,768]{1,0:T(8,128)(2,1)}, u32[]{:S(2)}, u32[]{:S(2)}) collective-permute-start(bf16[256,768]{1,0:T(8,128)(2,1)} %collective-permute-done), channel_id=1, source_target_pairs={{0,4},{4,8},{8,12},{12,16},{16,20},{20,24},{24,28},{28,0},{1,5},{5... | collective-permute-start | bytes 1179656 | tf_op jit(solution)/shard_map/ppermute | solution.py:21
  120.8 20.8 %copy-start.8 = (bf16[256,768]{1,0:T(8,128)(2,1)S(1)}, bf16[256,768]{1,0:T(8,128)(2,1)}, u32[]{:S(2)}) copy-start(bf16[256,768]{1,0:T(8,128)(2,1)} %get-tuple-element.261) | copy-start | bytes 1179652
  138.0 22.3 %collective-permute-start.4 = (bf16[256,768]{1,0:T(8,128)(2,1)}, bf16[256,768]{1,0:T(8,128)(2,1)}, u32[]{:S(2)}, u32[]{:S(2)}) collective-permute-start(bf16[256,768]{1,0:T(8,128)(2,1)} %collective-permute-done.2), channel_id=1, source_target_pairs={{0,4},{4,8},{8,12},{12,16},{16,20},{20,24},{24,28},{28,0},{1,5},{5... | collective-permute-start | bytes 1179656 | tf_op jit(solution)/shard_map/ppermute | solution.py:21
  142.5 5.5 copy-start.14
  150.0 31.7 %collective-permute-start.5 = (bf16[256,768]{1,0:T(8,128)(2,1)}, bf16[256,768]{1,0:T(8,128)(2,1)}, u32[]{:S(2)}, u32[]{:S(2)}) collective-permute-start(bf16[256,768]{1,0:T(8,128)(2,1)} %collective-permute-done.3), channel_id=1, source_target_pairs={{0,28},{4,0},{8,4},{12,8},{16,12},{20,16},{24,20},{28,24},{1,29},{... | collective-permute-start | bytes 1179656 | tf_op jit(solution)/shard_map/ppermute | solution.py:24
  160.3 25.9 %collective-permute-start.6 = (bf16[256,768]{1,0:T(8,128)(2,1)}, bf16[256,768]{1,0:T(8,128)(2,1)}, u32[]{:S(2)}, u32[]{:S(2)}) collective-permute-start(bf16[256,768]{1,0:T(8,128)(2,1)} %collective-permute-done.4), channel_id=1, source_target_pairs={{0,4},{4,8},{8,12},{12,16},{16,20},{20,24},{24,28},{28,0},{1,5},{5... | collective-permute-start | bytes 1179656 | tf_op jit(solution)/shard_map/ppermute | solution.py:21
  188.2 5.6 copy-start.13
  285.2 25.2 %copy-start.9 = (bf16[12,512,64]{1,2,0:T(8,128)(2,1)S(1)}, bf16[12,512,64]{1,2,0:T(8,128)(2,1)}, u32[]{:S(2)}) copy-start(bf16[12,512,64]{1,2,0:T(8,128)(2,1)} %get-tuple-element.103) | copy-start | bytes 2359300
  312.6 1.1 copy-start.2
  314.0 127.0 %copy-start.5 = (bf16[1,2,256,768]{3,2,1,0:T(8,128)(2,1)S(1)}, bf16[1,2,256,768]{3,2,1,0:T(8,128)(2,1)}, u32[]{:S(2)}) copy-start(bf16[1,2,256,768]{3,2,1,0:T(8,128)(2,1)} %param.31) | copy-start | bytes 2359300
  441.0 19.9 %copy-start.3 = (f32[512,768]{1,0:T(8,128)S(1)}, f32[512,768]{1,0:T(8,128)}, u32[]{:S(2)}) copy-start(f32[512,768]{1,0:T(8,128)} %copy-done.2) | copy-start | bytes 4718596
  441.0 19.9 %copy-start.36 = (bf16[768,3072]{1,0:T(8,128)(2,1)S(1)}, bf16[768,3072]{1,0:T(8,128)(2,1)}, u32[]{:S(2)}) copy-start(bf16[768,3072]{1,0:T(8,128)(2,1)} %all-gather.13.cloned.1.call-done) | copy-start | bytes 14155780
  460.8 3.4 copy-start.12
  464.3 3.1 copy-start.37
  464.9 1.2 copy-start
  466.4 0.9 copy-start.11
  629.2 151.6 %reduce-scatter.9.cloned.1.call-start = ((), (), s32[]{:S(2)}) async-start(), calls=%async_computation.13 | async-start | bytes 3538944 | tf_op jit(solution)/shard_map/reduce_scatter | solution.py:273
  633.2 1.1 copy-start.10
  633.2 4.6 copy-start.31
  633.2 251.7 %reduce-scatter.13.cloned.1.call-start = ((), (), s32[]{:S(2)}) async-start(), calls=%async_computation.15 | async-start | bytes 2433024 | tf_op jit(solution)/shard_map/reduce_scatter | solution.py:298
  637.8 389.0 %reduce-scatter.17.cloned.1.call-start = ((), (), s32[]{:S(2)}) async-start(), calls=%async_computation.17 | async-start | bytes 9732096 | tf_op jit(solution)/shard_map/reduce_scatter | solution.py:302
  647.8 1.4 copy-start.4
  647.9 519.9 %reduce-scatter.15.cloned.1.call-start = ((), (), s32[]{:S(2)}) async-start(), calls=%async_computation.16 | async-start | bytes 9732096 | tf_op jit(solution)/shard_map/reduce_scatter | solution.py:300
  656.4 47.7 %copy-start.18 = (f32[512,32]{0,1:T(8,128)S(1)}, f32[512,32]{0,1:T(8,128)}, u32[]{:S(2)}) copy-start(f32[512,32]{0,1:T(8,128)} %copy-done.17) | copy-start | bytes 196612
  656.4 47.7 %copy-start.20 = (f32[512,32]{0,1:T(8,128)S(1)}, f32[512,32]{0,1:T(8,128)}, u32[]{:S(2)}) copy-start(f32[512,32]{0,1:T(8,128)} %get-tuple-element.281) | copy-start | bytes 196612
  656.5 636.8 %reduce-scatter.11.cloned.1.call-start = ((), (), s32[]{:S(2)}) async-start(), calls=%async_computation.14 | async-start | bytes 7299072 | tf_op jit(solution)/shard_map/reduce_scatter | solution.py:297
  704.2 76.5 %copy-start.22 = (f32[512]{0:T(512)S(1)}, f32[512]{0:T(512)}, u32[]{:S(2)}) copy-start(f32[512]{0:T(512)} %copy-done.21) | copy-start | bytes 6148
  704.2 76.5 %copy-start.24 = (f32[512]{0:T(512)S(1)}, f32[512]{0:T(512)}, u32[]{:S(2)}) copy-start(f32[512]{0:T(512)} %copy-done.23) | copy-start | bytes 6148
  704.2 76.5 %copy-start.26 = (f32[768]{0:T(1024)S(1)}, f32[768]{0:T(1024)}, u32[]{:S(2)}) copy-start(f32[768]{0:T(1024)} %copy-done.25) | copy-start | bytes 9220
  706.5 74.3 %copy-start.19 = (bf16[256,12,64]{0,2,1:T(8,128)(2,1)S(1)}, bf16[256,12,64]{0,2,1:T(8,128)(2,1)}, u32[]{:S(2)}) copy-start(bf16[256,12,64]{0,2,1:T(8,128)(2,1)} %slice.124) | copy-start | bytes 1179652
  790.0 9.3 copy-start.7
  790.0 9.3 copy-start.15
  790.0 9.3 copy-start.16
  790.0 9.3 copy-start.38
  799.3 2.5 copy-start.28
  801.8 1.4 copy-start.1
  801.8 1.6 copy-start.6
  802.5 1.4 copy-start.34
  803.4 1.3 copy-start.29
  803.4 1.3 copy-start.30
  803.4 1.3 copy-start.32
Sparse Core Ops, SparseCore 0:
  10.9 62.8 all-gather.6
  90.0 103.8 all-gather.8
  196.1 58.7 all-gather.16
  257.6 52.7 all-gather.10
  313.1 62.5 all-gather.12
  378.5 62.4 all-gather.14
  629.3 73.7 reduce-scatter.6
  706.7 73.9 reduce-scatter.8
  786.6 98.1 reduce-scatter.12
  892.2 134.4 reduce-scatter.16
  1033.2 134.4 reduce-scatter.14
  1174.8 118.4 reduce-scatter.10
